TPU v7x, 128 devices: a whole 4x4x4 slice. The times are simulated.
128 devices in a mesh: dp: 16 (over y_hi, x, core), row: 4 (over z), col: 2 (over y_lo).
Axes of the slice: x: 4, y: 4 (y_hi: 2, y_lo: 2; y = y_hi * 2 + y_lo), z: 4, core: 2. Of those that a mesh axis runs over, the one named last changes fastest.
Arguments:
- x_in: bfloat16 [8192, 1024], P('dp', 'row'), may hold values from -24 to 24
- segments: int32 [16, 512], P('dp'), may hold values from 0 to 3, never falling along the last dimension, each value on 1 to 256 neighbouring positions
- expert_ids: int32 [8192, 8], P('dp'), may hold values from 0 to 31, all different within a row; in each aligned block of 512 rows (0 to 511, 512 to 1023, ...) at most 160 rows name the same one
- cotangent: bfloat16 [8192, 1024], P('dp', 'row'), may hold values from -6 to 6
- norm_gain1: float32 [1024], P('row'), may hold values from 0.5 to 1.5
- w_query: bfloat16 [1024, 1024], P('row', 'col'), may hold values from -12 to 12
- w_key: bfloat16 [1024, 512], P('row', 'col'), may hold values from -1 to 1
- w_value: bfloat16 [1024, 512], P('row', 'col'), may hold values from -0.1875 to 0.1875
- w_out: bfloat16 [1024, 1024], P('col', 'row'), may hold values from -1.5 to 1.5
- norm_gain2: float32 [1024], P('row'), may hold values from 0.5 to 1.5
- w_router: bfloat16 [1024, 32], P('row'), may hold values from -24 to 24
- w_gate: bfloat16 [32, 1024, 512], P(None, 'row', 'col'), may hold values from -0.1875 to 0.1875
- w_up: bfloat16 [32, 1024, 512], P(None, 'row', 'col'), may hold values from -0.1875 to 0.1875
- w_down: bfloat16 [32, 512, 1024], P(None, 'col', 'row'), may hold values from -0.25 to 0.25
Outputs:
- block_out: bfloat16 [8192, 1024], P('dp', 'row')
- grad_input: bfloat16 [8192, 1024], P('dp', 'row')
- grad_query: float32 [1024, 1024], P('row', 'col')
- grad_key: float32 [1024, 512], P('row', 'col')
- grad_value: float32 [1024, 512], P('row', 'col')
- grad_out: float32 [1024, 1024], P('col', 'row')
- grad_router: float32 [1024, 32], P('row')
- grad_gate: float32 [32, 1024, 512], P('dp', 'row', 'col')
- grad_up: float32 [32, 1024, 512], P('dp', 'row', 'col')
- grad_down: float32 [32, 512, 1024], P('dp', 'col', 'row')
- grad_gain1: float32 [1024], P('row')
- grad_gain2: float32 [1024], P('row')
Inputs may be any that keep to these rules, and one draw needn't show every extreme that they name: `expert_ids`: each token names 8 different experts; within one sequence no expert is named by more than 160 tokens, and in some sequence one is named by exactly 160. `segments`: segment numbers never fall along a sequence; a segment holds at most 256 tokens, and some segment holds exactly that many.
All inputs are finite; a program needn't handle non-finite values.
Results may differ from a plain program's by a relative error of at most 0.0117.
The roundings to bfloat16 on the way count: a program that leaves them out, or rounds other values in their place, can miss the bound.
Values may be sent and summed in bfloat16 or wider, within the bound.
A program may use at most 192 MiB of HBM per device.

v0:
```python
import jax
import jax.numpy as jnp
from jax import lax
from jax.sharding import PartitionSpec as P

D = 1024
HEAD_DIM = 64
EXPERTS = 32
TOPK = 8
CAP = 160
EPSILON = 1e-06
ROPE_BASE = 10000.0
MASKED = -1e30


def rope_tables(positions):
    half_dim = HEAD_DIM // 2
    exponent = jnp.arange(half_dim).astype(jnp.float32) * (2.0 / HEAD_DIM)
    angles = positions.astype(jnp.float32)[:, None] * (ROPE_BASE ** (-exponent))[None, :]
    return (jnp.cos(angles)[:, None, :], jnp.sin(angles)[:, None, :])


def rotate(values_in, cosine, sine_part):
    half_dim = values_in.shape[-1] // 2
    low_half = values_in[..., :half_dim]
    high_half = values_in[..., half_dim:]
    return jnp.concatenate(
        [low_half * cosine - high_half * sine_part, high_half * cosine + low_half * sine_part],
        axis=-1,
    )


def slot_tables(route_rows):
    count_pairs = route_rows.shape[0] * route_rows.shape[1]
    flat_routes = route_rows.reshape(-1)
    expert_hits = (flat_routes[:, None] == jnp.arange(EXPERTS, dtype=jnp.int32)[None, :]).astype(
        jnp.int32
    )
    running = jnp.cumsum(expert_hits, axis=0)
    before = jnp.sum((running - 1) * expert_hits, axis=1)
    slot_of = flat_routes * CAP + before
    pair_of = (
        jnp.full((EXPERTS * CAP,), count_pairs, jnp.int32)
        .at[slot_of]
        .set(jnp.arange(count_pairs, dtype=jnp.int32))
    )
    return (slot_of, pair_of)


def row_total(vector):
    return lax.psum(vector, "row")


def col_total(matrix):
    return lax.psum(matrix, "col")


def head_share(matrix):
    return lax.psum_scatter(matrix, "row", scatter_dimension=0, tiled=True)


def head_collect(matrix):
    return lax.all_gather(matrix, "row", axis=0, tiled=True)


def slot_share(matrix):
    return lax.psum_scatter(matrix, "row", scatter_dimension=0, tiled=True)


def slot_collect(matrix):
    return lax.all_gather(matrix, "row", axis=0, tiled=True)


def norm_inverse(residual):
    squares = row_total(jnp.sum(residual * residual, axis=1))
    return lax.rsqrt(squares / D + EPSILON)[:, None]


def norm_backward(residual, inverse, gain, grad_normed):
    weighted = grad_normed * gain
    project = (row_total(jnp.sum(weighted * residual, axis=1)) / D)[:, None]
    grad_residual = inverse * weighted - residual * inverse**3 * project
    grad_gain = jnp.sum(grad_normed * residual * inverse, axis=0)
    return (grad_residual, grad_gain)


def on_device(
    x_in,
    segments,
    expert_ids,
    cotangent,
    norm_gain1,
    w_query,
    w_key,
    w_value,
    w_out,
    norm_gain2,
    w_router,
    w_gate,
    w_up,
    w_down,
):
    f32 = jnp.float32
    low = jnp.bfloat16
    length = x_in.shape[0]
    feature_part = x_in.shape[1]
    quarters = lax.axis_size("row")
    own_rows = length // quarters
    own_start = lax.axis_index("row") * own_rows
    query_width = w_query.shape[1]
    key_width = w_key.shape[1]
    heads_here = query_width // HEAD_DIM
    key_heads = key_width // HEAD_DIM
    group_size = heads_here // key_heads
    score_scale = HEAD_DIM ** (-0.5)
    residual = x_in.astype(f32)
    scale_attn = norm_inverse(residual)
    normed_attn = (residual * scale_attn * norm_gain1).astype(low)
    joined_proj = jnp.concatenate([w_query, w_key, w_value], axis=1)
    projected = head_share(jnp.dot(normed_attn, joined_proj, preferred_element_type=f32))
    positions = own_start + jnp.arange(own_rows, dtype=jnp.int32)
    cosine, sine_part = rope_tables(positions)
    queries = rotate(
        projected[:, :query_width].reshape(own_rows, heads_here, HEAD_DIM), cosine, sine_part
    ).astype(low)
    own_keys = rotate(
        projected[:, query_width : query_width + key_width].reshape(own_rows, key_heads, HEAD_DIM),
        cosine,
        sine_part,
    ).astype(low)
    own_values = projected[:, query_width + key_width :].astype(low)
    key_value = head_collect(
        jnp.concatenate([own_keys.reshape(own_rows, key_width), own_values], axis=1)
    )
    keys_wide = jnp.repeat(
        key_value[:, :key_width].reshape(length, key_heads, HEAD_DIM), group_size, axis=1
    )
    values_wide = jnp.repeat(
        key_value[:, key_width:].reshape(length, key_heads, HEAD_DIM), group_size, axis=1
    )
    segment_all = segments.reshape(-1)
    key_places = jnp.arange(length, dtype=jnp.int32)
    block_rows = min(256, own_rows)
    blocks = own_rows // block_rows
    query_blocks = queries.reshape(blocks, block_rows, heads_here, HEAD_DIM)
    place_blocks = positions.reshape(blocks, block_rows)
    segment_blocks = lax.dynamic_slice_in_dim(segment_all, own_start, own_rows).reshape(
        blocks, block_rows
    )

    def block_scores(query_block, place_block, segment_block):
        scores = (
            jnp.einsum("qhd,khd->hqk", query_block, keys_wide, preferred_element_type=f32)
            * score_scale
        )
        allowed = (key_places[None, :] <= place_block[:, None]) & (
            segment_all[None, :] == segment_block[:, None]
        )
        return jnp.where(allowed[None], scores, MASKED)

    def forward_block(unused_carry, inputs):
        query_block, place_block, segment_block = inputs
        scores = block_scores(query_block, place_block, segment_block)
        top_score = jnp.max(scores, axis=2, keepdims=True)
        log_total = top_score + jnp.log(jnp.sum(jnp.exp(scores - top_score), axis=2, keepdims=True))
        weights_low = jnp.exp(scores - log_total).astype(low)
        attended = jnp.einsum(
            "hqk,khd->qhd", weights_low, values_wide, preferred_element_type=f32
        ).astype(low)
        return (unused_carry, (attended, log_total))

    _, (attended_blocks, total_blocks) = lax.scan(
        forward_block, jnp.zeros((), jnp.int32), (query_blocks, place_blocks, segment_blocks)
    )
    attended_all = head_collect(attended_blocks.reshape(own_rows, query_width))
    resid_mid = residual + col_total(jnp.dot(attended_all, w_out, preferred_element_type=f32))
    scale_ffn = norm_inverse(resid_mid)
    normed_ffn = (resid_mid * scale_ffn * norm_gain2).astype(low)
    logits = lax.psum(jnp.dot(normed_ffn, w_router, preferred_element_type=f32), "row")
    gate_probs = jax.nn.softmax(jnp.take_along_axis(logits, expert_ids, axis=1), axis=1)
    slot_of, pair_of = slot_tables(expert_ids)
    owner_row = pair_of // TOPK
    padded = jnp.concatenate([normed_ffn, jnp.zeros((1, feature_part), low)], axis=0)
    dispatched = jnp.take(padded, owner_row, axis=0).reshape(EXPERTS, CAP, feature_part)
    both_weights = jnp.concatenate([w_gate, w_up], axis=2)
    hidden_width = w_gate.shape[2]
    pre_act = jnp.einsum("ecd,edf->ecf", dispatched, both_weights, preferred_element_type=f32)
    pre_own = slot_share(pre_act.reshape(EXPERTS * CAP, 2 * hidden_width))
    gate_act = pre_own[:, :hidden_width]
    up_act = pre_own[:, hidden_width:]
    sigmoid_gate = jax.nn.sigmoid(gate_act)
    hidden_own = (gate_act * sigmoid_gate * up_act).astype(low)
    hidden_all = slot_collect(hidden_own).reshape(EXPERTS, CAP, hidden_width)
    expert_out = jnp.einsum("ecf,efd->ecd", hidden_all, w_down, preferred_element_type=f32).reshape(
        EXPERTS * CAP, feature_part
    )
    picked = jnp.take(expert_out, slot_of, axis=0).reshape(length, TOPK, feature_part)
    resid_out = resid_mid + col_total(jnp.sum(gate_probs[:, :, None] * picked, axis=1))
    block_out = resid_out.astype(low)
    grad_top = cotangent.astype(f32)
    grad_prob = lax.psum(jnp.sum(grad_top[:, None, :] * picked, axis=2), ("row", "col"))
    grad_chosen = gate_probs * (grad_prob - jnp.sum(gate_probs * grad_prob, axis=1, keepdims=True))
    expert_hits = (
        expert_ids[:, :, None] == jnp.arange(EXPERTS, dtype=jnp.int32)[None, None, :]
    ).astype(f32)
    grad_logits = jnp.sum(expert_hits * grad_chosen[:, :, None], axis=1).astype(low)
    grad_router = jnp.dot(normed_ffn.T, grad_logits, preferred_element_type=f32)
    spread = (gate_probs[:, :, None] * grad_top[:, None, :]).reshape(length * TOPK, feature_part)
    spread = jnp.concatenate([spread, jnp.zeros((1, feature_part), f32)], axis=0)
    slot_grad = jnp.take(spread, pair_of, axis=0).astype(low).reshape(EXPERTS, CAP, feature_part)
    hidden_grad = slot_share(
        jnp.einsum("ecd,efd->ecf", slot_grad, w_down, preferred_element_type=f32).reshape(
            EXPERTS * CAP, hidden_width
        )
    )
    grad_pre = jnp.concatenate(
        [
            hidden_grad * up_act * sigmoid_gate * (1.0 + gate_act * (1.0 - sigmoid_gate)),
            hidden_grad * gate_act * sigmoid_gate,
        ],
        axis=1,
    ).astype(low)
    grad_pre_all = slot_collect(grad_pre).reshape(EXPERTS, CAP, 2 * hidden_width)
    slot_input = jnp.einsum(
        "ecf,edf->ecd", grad_pre_all, both_weights, preferred_element_type=f32
    ).reshape(EXPERTS * CAP, feature_part)
    grad_both_full = jnp.einsum(
        "ecd,ecf->edf", dispatched, grad_pre_all, preferred_element_type=f32
    )
    grad_down_full = jnp.einsum("ecf,ecd->efd", hidden_all, slot_grad, preferred_element_type=f32)
    grad_both, grad_down = (
        lax.psum_scatter(grad_both_full, "dp", scatter_dimension=0, tiled=True),
        lax.psum_scatter(grad_down_full, "dp", scatter_dimension=0, tiled=True),
    )
    grad_gate = grad_both[:, :, :hidden_width]
    grad_up = grad_both[:, :, hidden_width:]
    token_grad = jnp.sum(
        jnp.take(slot_input, slot_of, axis=0).reshape(length, TOPK, feature_part), axis=1
    )
    grad_normed_ffn = col_total(token_grad) + jnp.dot(
        grad_logits, w_router.T, preferred_element_type=f32
    )
    grad_ffn_in, grad_gain2 = norm_backward(resid_mid, scale_ffn, norm_gain2, grad_normed_ffn)
    grad_mid = grad_top + grad_ffn_in
    grad_mid_low = grad_mid.astype(low)
    grad_out_part = jnp.dot(attended_all.T, grad_mid_low, preferred_element_type=f32)
    grad_attended = head_share(jnp.dot(grad_mid_low, w_out.T, preferred_element_type=f32)).astype(
        low
    )
    grad_blocks = grad_attended.reshape(blocks, block_rows, heads_here, HEAD_DIM)

    def backward_block(carry, inputs):
        key_acc, value_acc = carry
        query_block, place_block, segment_block, attended_block, total_block, grad_block = inputs
        scores = block_scores(query_block, place_block, segment_block)
        weights = jnp.exp(scores - total_block)
        value_step = jnp.einsum(
            "hqk,qhd->khd", weights.astype(low), grad_block, preferred_element_type=f32
        )
        grad_weights = jnp.einsum(
            "qhd,khd->hqk", grad_block, values_wide, preferred_element_type=f32
        )
        delta_sum = jnp.sum(grad_block.astype(f32) * attended_block.astype(f32), axis=2).T[
            :, :, None
        ]
        grad_scores = (weights * (grad_weights - delta_sum)).astype(low)
        grad_query_block = (
            jnp.einsum("hqk,khd->qhd", grad_scores, keys_wide, preferred_element_type=f32)
            * score_scale
        )
        key_step = (
            jnp.einsum("hqk,qhd->khd", grad_scores, query_block, preferred_element_type=f32)
            * score_scale
        )
        return ((key_acc + key_step, value_acc + value_step), grad_query_block)

    zeros_wide = jnp.zeros((length, heads_here, HEAD_DIM), f32)
    (key_acc, value_acc), grad_query_blocks = lax.scan(
        backward_block,
        (zeros_wide, zeros_wide),
        (query_blocks, place_blocks, segment_blocks, attended_blocks, total_blocks, grad_blocks),
    )
    key_partial = jnp.sum(key_acc.reshape(length, key_heads, group_size, HEAD_DIM), axis=2).reshape(
        length, key_width
    )
    value_partial = jnp.sum(
        value_acc.reshape(length, key_heads, group_size, HEAD_DIM), axis=2
    ).reshape(length, key_width)
    key_value_grad = head_share(jnp.concatenate([key_partial, value_partial], axis=1))
    grad_queries = (
        rotate(grad_query_blocks.reshape(own_rows, heads_here, HEAD_DIM), cosine, -sine_part)
        .astype(low)
        .reshape(own_rows, query_width)
    )
    grad_keys = (
        rotate(
            key_value_grad[:, :key_width].reshape(own_rows, key_heads, HEAD_DIM), cosine, -sine_part
        )
        .astype(low)
        .reshape(own_rows, key_width)
    )
    grad_values = key_value_grad[:, key_width:].astype(low)
    grad_proj = head_collect(jnp.concatenate([grad_queries, grad_keys, grad_values], axis=1))
    grad_joined = jnp.dot(normed_attn.T, grad_proj, preferred_element_type=f32)
    grad_normed_attn = col_total(jnp.dot(grad_proj, joined_proj.T, preferred_element_type=f32))
    grad_attn_in, grad_gain1 = norm_backward(residual, scale_attn, norm_gain1, grad_normed_attn)
    grad_input = (grad_mid + grad_attn_in).astype(low)
    joined_sum, out_sum, router_sum, gain1_sum, gain2_sum = lax.psum(
        (grad_joined, grad_out_part, grad_router, grad_gain1, grad_gain2), "dp"
    )
    return (
        block_out,
        grad_input,
        joined_sum[:, :query_width],
        joined_sum[:, query_width : query_width + key_width],
        joined_sum[:, query_width + key_width :],
        out_sum,
        router_sum,
        grad_gate,
        grad_up,
        grad_down,
        gain1_sum,
        gain2_sum,
    )


def solution(mesh):
    placed = (
        P("dp", "row"),
        P("dp", None),
        P("dp", None),
        P("dp", "row"),
        P("row"),
        P("row", "col"),
        P("row", "col"),
        P("row", "col"),
        P("col", "row"),
        P("row"),
        P("row", None),
        P(None, "row", "col"),
        P(None, "row", "col"),
        P(None, "col", "row"),
    )
    return jax.shard_map(
        on_device,
        mesh=mesh,
        in_specs=placed,
        out_specs=(
            P("dp", "row"),
            P("dp", "row"),
            P("row", "col"),
            P("row", "col"),
            P("row", "col"),
            P("col", "row"),
            P("row", None),
            P("dp", "row", "col"),
            P("dp", "row", "col"),
            P("dp", "col", "row"),
            P("row"),
            P("row"),
        ),
        check_vma=False,
    )
```

profile of v0, /device:TPU:0, one launch (start us, length us, event | category | flops | bytes accessed | tf_op | source)
XLA Modules:
  0.0 1184.1 jit_solution(17169282977297748467)
XLA Ops:
  8.4 11.9 %psum.105 = f32[512]{0:T(512)S(1)} all-reduce(f32[512]{0:T(512)S(1)} %fusion.10), channel_id=1, replica_groups=mesh['dp'=16,'row'=4,'col'=2] {'row'}, use_global_device_ids=true, to_apply=%region_1.0 | all-reduce | flops 512 | bytes 4096 | tf_op jit(solution)/shard_map/psum | solution.py:51
  28.1 9.2 reduce-window.6
  38.9 15.5 %scatter_custom_fusion = s32[5120]{0:T(1024)S(1)} fusion(s32[4096]{0:T(1024)S(1)} %bitcast.134, s32[4096]{0:T(1024)S(1)} %iota.35, s32[]{:T(128)} %constant.152.clone.1), kind=kCustom, calls=%fused_computation.130 | custom fusion | bytes 20484 | tf_op jit(solution)/shard_map/scatter | solution.py:45
  59.8 13.5 %all_gather.15 = bf16[512,512]{1,0:T(8,128)(2,1)S(1)} all-gather(bf16[128,512]{1,0:T(8,128)(2,1)S(1)} %pad_maximum_fusion.3), channel_id=1, replica_groups=mesh['dp'=16,'row'=4,'col'=2] {'row'}, dimensions={0}, use_global_device_ids=true | all-gather | bytes 655360 | tf_op jit(solution)/shard_map/all_gather | solution.py:63
  76.6 13.0 %all_gather.16 = bf16[512,512]{0,1:T(8,128)(2,1)S(1)} all-gather(bf16[128,512]{0,1:T(8,128)(2,1)S(1)} %bitcast.123), channel_id=1, replica_groups=mesh['dp'=16,'row'=4,'col'=2] {'row'}, dimensions={0}, use_global_device_ids=true | all-gather | bytes 655360 | tf_op jit(solution)/shard_map/all_gather | solution.py:63
  101.2 26.6 %all-reduce.11.cloned.1.call-done = f32[512,256]{1,0:T(8,128)} async-done(((f32[512,256]{1,0:T(8,128)}), f32[512,256]{1,0:T(8,128)}) %all-reduce.11.cloned.1.call-update) | async-done | bytes 524304 | tf_op jit(solution)/shard_map/psum | solution.py:55
  129.0 10.7 psum.107
  140.5 18.2 %gather_fusion = bf16[5120,256]{1,0:T(8,128)(2,1)S(1)} fusion(bf16[513,256]{1,0:T(8,128)(2,1)S(1)} %concatenate.45, s32[5120]{0:T(1024)S(1)} %get-tuple-element.121), kind=kCustom, calls=%fused_computation.2 | custom fusion | bytes 5263360 | tf_op jit(solution)/shard_map/jit(_take)/gather | solution.py:184
  158.7 8.1 fusion.3
  168.4 95.0 %reduce-scatter.10.cloned.1.call-done = f32[1280,512]{1,0:T(8,128)} async-done(((f32[5120,512]{1,0:T(8,128)}), f32[1280,512]{1,0:T(8,128)}) %reduce-scatter.10.cloned.1.call-update) | async-done | bytes 2621456 | tf_op jit(solution)/shard_map/reduce_scatter | solution.py:67
  267.0 39.8 %all-reduce.13.cloned.1.call-done = f32[512,32]{0,1:T(8,128)} async-done(((f32[512,32]{0,1:T(8,128)}), f32[512,32]{0,1:T(8,128)}) %all-reduce.13.cloned.1.call-update) | async-done | bytes 65552 | tf_op jit(solution)/shard_map/psum | solution.py:179
  306.8 28.9 %gather_fusion.2 = f32[4096]{0:T(1024)S(1)} fusion(f32[512,32]{0,1:T(8,128)} %all-reduce.13.cloned.1.call-done, s32[4096]{0:T(1024)S(1)} %reshape.440), kind=kCustom, calls=%fused_computation.4 | custom fusion | bytes 65536 | tf_op jit(solution)/shard_map/jit(take_along_axis)/gather | solution.py:180
  336.0 8.1 all-gather.4.cloned.1.call-done
  350.3 18.7 %gather_fusion.3 = f32[4096,256]{1,0:T(8,128)} fusion(f32[5120,256]{1,0:T(8,128)} %bitcast.103, s32[4096]{0:T(1024)S(1)} %broadcast_clamp_fusion.1), kind=kCustom, calls=%fused_computation.clone | custom fusion | bytes 8404992 | tf_op jit(solution)/shard_map/jit(_take)/gather | solution.py:197
  372.1 32.4 %psum.111 = f32[512,8]{0,1:T(8,128)S(1)} all-reduce(f32[512,8]{0,1:T(8,128)S(1)} %copy.81), channel_id=1, replica_groups=mesh['dp'=16,'row'=4,'col'=2] {'row','col'}, use_global_device_ids=true, to_apply=%region_22.24 | all-reduce | flops 4096 | bytes 32768 | tf_op jit(solution)/shard_map/psum | solution.py:201
  406.7 21.0 %gather_fusion.1 = bf16[5120,256]{1,0:T(8,128)(2,1)} fusion(bf16[4097,256]{1,0:T(8,128)(2,1)S(1)} %concatenate.47, s32[5120]{0:T(1024)S(1)} %get-tuple-element.120), kind=kCustom, calls=%fused_computation.3 | custom fusion | bytes 5263360 | tf_op jit(solution)/shard_map/jit(_take)/gather | solution.py:210
  434.7 54.1 %reduce-scatter.12.cloned.1.call-done = f32[1280,256]{1,0:T(8,128)} async-done(((f32[5120,256]{1,0:T(8,128)}), f32[1280,256]{1,0:T(8,128)}) %reduce-scatter.12.cloned.1.call-update) | async-done | bytes 1310736 | tf_op jit(solution)/shard_map/reduce_scatter | solution.py:67
  492.0 56.9 %all-gather.6.cloned.1.call-done = bf16[5120,512]{1,0:T(8,128)(2,1)} async-done(((bf16[1280,512]{1,0:T(8,128)(2,1)}), bf16[5120,512]{1,0:T(8,128)(2,1)}) %all-gather.6.cloned.1.call-update) | async-done | bytes 5242896 | tf_op jit(solution)/shard_map/all_gather | solution.py:71
  548.9 10.1 fusion.64
  559.0 18.7 %gather_fusion.4 = f32[4096,256]{1,0:T(8,128)} fusion(f32[5120,256]{1,0:T(8,128)} %bitcast.102, s32[4096]{0:T(1024)S(1)} %broadcast_clamp_fusion.1), kind=kCustom, calls=%fused_computation.1.clone | custom fusion | bytes 8404992 | tf_op jit(solution)/shard_map/jit(_take)/gather | solution.py:238
  585.7 35.5 %all-reduce.15.cloned.1.call-done = f32[512,256]{1,0:T(8,128)} async-done(((f32[512,256]{1,0:T(8,128)}), f32[512,256]{1,0:T(8,128)}) %all-reduce.15.cloned.1.call-update) | async-done | bytes 524304 | tf_op jit(solution)/shard_map/psum | solution.py:55
  624.0 10.6 psum.112
  637.8 22.3 %reduce-scatter.14.cloned.1.call-done = f32[128,512]{1,0:T(8,128)} async-done(((f32[512,512]{1,0:T(8,128)}), f32[128,512]{1,0:T(8,128)}) %reduce-scatter.14.cloned.1.call-update) | async-done | bytes 262160 | tf_op jit(solution)/shard_map/reduce_scatter | solution.py:59
  669.3 22.4 %reduce-scatter.16.cloned.1.call-done = f32[128,512]{0,1:T(8,128)} async-done(((f32[512,512]{0,1:T(8,128)}), f32[128,512]{0,1:T(8,128)}) %reduce-scatter.16.cloned.1.call-update) | async-done | bytes 262160 | tf_op jit(solution)/shard_map/reduce_scatter | solution.py:59
  694.3 25.7 %all-gather.8.cloned.1.call-done = bf16[512,1024]{0,1:T(8,128)(2,1)} async-done(((bf16[128,1024]{0,1:T(8,128)(2,1)}), bf16[512,1024]{0,1:T(8,128)(2,1)}) %all-gather.8.cloned.1.call-update) | async-done | bytes 1048592 | tf_op jit(solution)/shard_map/all_gather | solution.py:63
  728.1 9.1 fusion.2
  745.7 25.5 %all-reduce.19.cloned.1.call-done = (f32[512,256]{1,0:T(8,128)}, f32[512,256]{1,0:T(8,128)}) async-done(((f32[512,256]{1,0:T(8,128)}, f32[512,256]{1,0:T(8,128)}), (f32[512,256]{1,0:T(8,128)}, f32[512,256]{1,0:T(8,128)})) %all-reduce.19.cloned.1.call-update) | async-done | bytes 1048592 | tf_op jit(solution)/shard_map/psum | solution.py:55
  772.5 10.7 psum.114
  783.2 67.6 %all-reduce.2 = (f32[256,32]{0,1:T(8,128)}, f32[256]{0:T(256)}, f32[256]{0:T(256)}) all-reduce(f32[256,32]{0,1:T(8,128)S(1)} %fusion.66, f32[256]{0:T(256)S(1)} %get-tuple-element.73, f32[256]{0:T(256)S(1)} %copy-done.50), channel_id=1, replica_groups=mesh['dp'=16,'row'=4,'col'=2] {'dp'}, use_global_device_ids=true, to_apply=%region_37.39 | all-reduce | flops 8704 | bytes 69632 | tf_op jit(solution)/shard_map/psum | solution.py:308
  854.7 63.4 %all-reduce.17.cloned.1.call-done = (f32[256,1024]{1,0:T(8,128)}, f32[512,256]{1,0:T(8,128)}) async-done(((f32[256,1024]{1,0:T(8,128)}, f32[512,256]{1,0:T(8,128)}), (f32[256,1024]{1,0:T(8,128)}, f32[512,256]{1,0:T(8,128)})) %all-reduce.17.cloned.1.call-update) | async-done | bytes 1572880 | tf_op jit(solution)/shard_map/psum | solution.py:308
  921.8 149.2 %reduce-scatter.18.cloned.1.call-done = f32[2,256,512]{2,1,0:T(8,128)} async-done(((f32[32,256,512]{2,1,0:T(8,128)}), f32[2,256,512]{2,1,0:T(8,128)}) %reduce-scatter.18.cloned.1.call-update) | async-done | bytes 1048592 | tf_op jit(solution)/shard_map/reduce_scatter | solution.py:232
  1073.3 103.5 %reduce-scatter.20.cloned.1.call-done = f32[2,256,256]{2,1,0:T(8,128)} async-done(((f32[32,256,256]{2,1,0:T(8,128)}), f32[2,256,256]{2,1,0:T(8,128)}) %reduce-scatter.20.cloned.1.call-update) | async-done | bytes 524304 | tf_op jit(solution)/shard_map/reduce_scatter | solution.py:233
  (248 shorter events, 113.4 us)
Async XLA Ops:
  7.2 83.3 %copy-start = (bf16[512,256]{1,0:T(8,128)(2,1)S(1)}, bf16[512,256]{1,0:T(8,128)(2,1)}, u32[]{:S(2)}) copy-start(bf16[512,256]{1,0:T(8,128)(2,1)} %param.24) | copy-start | bytes 786436
  7.2 49.3 %reduce-scatter.8.cloned.1.call-start = ((), (), s32[]{:S(2)}) async-start(), calls=%async_computation.7 | async-start | bytes 2621440 | tf_op jit(solution)/shard_map/reduce_scatter | solution.py:59
  27.2 100.6 %all-reduce.11.cloned.1.call-start = ((), (), s32[]{:S(2)}) async-start(), calls=%async_computation.8 | async-start | bytes 1048576 | tf_op jit(solution)/shard_map/psum | solution.py:55
  91.7 171.7 %reduce-scatter.10.cloned.1.call-start = ((), (), s32[]{:S(2)}) async-start(), calls=%async_computation.10 | async-start | bytes 13107200 | tf_op jit(solution)/shard_map/reduce_scatter | solution.py:67
  96.5 31.3 %copy-start.9 = (bf16[512,256]{1,0:T(8,128)(2,1)S(1)}, bf16[512,256]{1,0:T(8,128)(2,1)}, u32[]{:S(2)}) copy-start(bf16[512,256]{1,0:T(8,128)(2,1)} %param.16) | copy-start | bytes 786436
  96.5 43.8 %copy-start.45 = (f32[256]{0:T(256)S(1)}, f32[256]{0:T(256)}, u32[]{:S(2)}) copy-start(f32[256]{0:T(256)} %param.25) | copy-start | bytes 3076
  166.8 100.1 %copy-start.27 = (bf16[512,256]{1,0:T(8,128)(2,1)S(1)}, bf16[512,256]{1,0:T(8,128)(2,1)}, u32[]{:S(2)}) copy-start(bf16[512,256]{1,0:T(8,128)(2,1)} %param.19) | copy-start | bytes 786436
  166.8 140.0 %all-reduce.13.cloned.1.call-start = ((), (), s32[]{:S(2)}) async-start(), calls=%async_computation.9 | async-start | bytes 131072 | tf_op jit(solution)/shard_map/psum | solution.py:179
  168.3 175.8 %all-gather.4.cloned.1.call-start = ((), (), s32[]{:S(2)}) async-start(), calls=%async_computation.11 | async-start | bytes 3276800 | tf_op jit(solution)/shard_map/all_gather | solution.py:71
  266.3 222.5 %reduce-scatter.12.cloned.1.call-start = ((), (), s32[]{:S(2)}) async-start(), calls=%async_computation.12 | async-start | bytes 6553600 | tf_op jit(solution)/shard_map/reduce_scatter | solution.py:67
  434.6 54.2 %copy-start.8 = (f32[1280,512]{1,0:T(8,128)S(1)}, f32[1280,512]{1,0:T(8,128)}, u32[]{:S(2)}) copy-start(f32[1280,512]{1,0:T(8,128)} %reduce-scatter.10.cloned.1.call-done) | copy-start | bytes 7864324
  434.7 114.2 %all-gather.6.cloned.1.call-start = ((), (), s32[]{:S(2)}) async-start(), calls=%async_computation.13 | async-start | bytes 6553600 | tf_op jit(solution)/shard_map/all_gather | solution.py:71
  491.9 129.3 %all-reduce.15.cloned.1.call-start = ((), (), s32[]{:S(2)}) async-start(), calls=%async_computation.14 | async-start | bytes 1048576 | tf_op jit(solution)/shard_map/psum | solution.py:55
  577.7 43.5 %copy-start.7 = (f32[512,256]{1,0:T(8,128)S(1)}, f32[512,256]{1,0:T(8,128)}, u32[]{:S(2)}) copy-start(f32[512,256]{1,0:T(8,128)} %copy-done.6) | copy-start | bytes 1572868
  577.7 43.5 %copy-start.46 = (f32[256]{0:T(256)S(1)}, f32[256]{0:T(256)}, u32[]{:S(2)}) copy-start(f32[256]{0:T(256)} %param.25) | copy-start | bytes 3076
  577.7 56.9 %copy-start.49 = (f32[512]{0:T(512)S(1)}, f32[512]{0:T(512)}, u32[]{:S(2)}) copy-start(f32[512]{0:T(512)} %get-tuple-element.124) | copy-start | bytes 6148
  585.6 74.5 %reduce-scatter.14.cloned.1.call-start = ((), (), s32[]{:S(2)}) async-start(), calls=%async_computation.15 | async-start | bytes 1310720 | tf_op jit(solution)/shard_map/reduce_scatter | solution.py:59
  585.7 48.9 %copy-start.36 = (bf16[512,32]{0,1:T(8,128)(2,1)}, bf16[512,32]{0,1:T(8,128)(2,1)S(1)}, u32[]{:S(2)}) copy-start(bf16[512,32]{0,1:T(8,128)(2,1)S(1)} %select_reduce_fusion) | copy-start | bytes 98308
  634.6 29.2 %copy-start.2 = (f32[8,128,512]{2,1,0:T(8,128)S(1)}, f32[8,128,512]{2,1,0:T(8,128)}, u32[]{:S(2)}) copy-start(f32[8,128,512]{2,1,0:T(8,128)} %copy-done.1) | copy-start | bytes 6291460
  637.5 54.1 %reduce-scatter.16.cloned.1.call-start = ((), (), s32[]{:S(2)}) async-start(), calls=%async_computation.16 | async-start | bytes 1310720 | tf_op jit(solution)/shard_map/reduce_scatter | solution.py:59
  668.2 51.8 %copy-start.23 = (bf16[256,1024]{1,0:T(8,128)(2,1)S(1)}, bf16[256,1024]{1,0:T(8,128)(2,1)}, u32[]{:S(2)}) copy-start(bf16[256,1024]{1,0:T(8,128)(2,1)} %copy-done.22) | copy-start | bytes 1572868
  668.2 51.8 %all-gather.8.cloned.1.call-start = ((), (), s32[]{:S(2)}) async-start(), calls=%async_computation.17 | async-start | bytes 1310720 | tf_op jit(solution)/shard_map/all_gather | solution.py:63
  694.2 30.8 %copy-start.43 = (f32[512]{0:T(512)S(1)}, f32[512]{0:T(512)}, u32[]{:S(2)}) copy-start(f32[512]{0:T(512)} %copy-done.42) | copy-start | bytes 6148
  694.2 30.8 %copy-start.44 = (f32[256]{0:T(256)S(1)}, f32[256]{0:T(256)}, u32[]{:S(2)}) copy-start(f32[256]{0:T(256)} %param.20) | copy-start | bytes 3076
  694.3 76.9 %all-reduce.19.cloned.1.call-start = ((), (), s32[]{:S(2)}) async-start(), calls=%async_computation.21 | async-start | bytes 2097152 | tf_op jit(solution)/shard_map/psum | solution.py:55
  722.5 195.5 %all-reduce.17.cloned.1.call-start = ((), (), s32[]{:S(2)}) async-start(), calls=%async_computation.20 | async-start | bytes 3145728 | tf_op jit(solution)/shard_map/psum | solution.py:308
  728.0 343.0 %reduce-scatter.18.cloned.1.call-start = ((), (), s32[]{:S(2)}) async-start(), calls=%async_computation.18 | async-start | bytes 17825792 | tf_op jit(solution)/shard_map/reduce_scatter | solution.py:232
  737.1 439.7 %reduce-scatter.20.cloned.1.call-start = ((), (), s32[]{:S(2)}) async-start(), calls=%async_computation.19 | async-start | bytes 8912896 | tf_op jit(solution)/shard_map/reduce_scatter | solution.py:233
  744.6 38.6 %copy-start.50 = (f32[256]{0:T(256)S(1)}, f32[256]{0:T(256)}, u32[]{:S(2)}) copy-start(f32[256]{0:T(256)} %get-tuple-element.71) | copy-start | bytes 3076
  744.6 108.1 %copy-start.47 = (f32[512]{0:T(512)S(1)}, f32[512]{0:T(512)}, u32[]{:S(2)}) copy-start(f32[512]{0:T(512)} %get-tuple-element.122) | copy-start | bytes 6148
  745.5 107.1 %copy-start.14 = (f32[512,256]{1,0:T(8,128)S(1)}, f32[512,256]{1,0:T(8,128)}, u32[]{:S(2)}) copy-start(f32[512,256]{1,0:T(8,128)} %copy-done.13) | copy-start | bytes 1572868
  918.0 258.7 %copy-start.33 = (f32[512,256]{1,0:T(8,128)S(1)}, f32[512,256]{1,0:T(8,128)}, u32[]{:S(2)}) copy-start(f32[512,256]{1,0:T(8,128)} %get-tuple-element.139) | copy-start | bytes 1572868
  (35 other events, 263.0 us)
Sparse Core Ops, SparseCore 0:
  27.3 29.1 reduce-scatter.7
  91.8 35.9 all-reduce.10
  166.9 96.3 reduce-scatter.9
  266.1 40.6 all-reduce.12
  308.4 35.6 all-gather.3
  434.8 53.9 reduce-scatter.11
  492.1 56.7 all-gather.5
  585.7 35.5 all-reduce.14
  637.6 22.4 reduce-scatter.13
  668.3 23.2 reduce-scatter.15
  694.4 25.5 all-gather.7
  723.5 47.6 all-reduce.18
  774.5 143.4 all-reduce.16
  922.3 148.7 reduce-scatter.17
  1076.4 100.3 reduce-scatter.19
where the time goes:
time: 1190 us; the launch traced here: 1180 us
  waiting for transfers between devices  729 us (61%)
  blocking collectives  170 us (14%)
  local copies, waits for them, and re-layouts  157 us (13%)
  matrix products  66.7 us (6%)
  other arithmetic  44.7 us (4%)
  between operations  14.9 us (1%)
    reduce_scatter x1, waiting for transfers between devices, on_device(): lax.psum_scatter(grad_both_full, 'dp', scatter_dimension=0, tiled=True)  149 us
    reduce_scatter x2, waiting for transfers between devices, slot_share(): return lax.psum_scatter(matrix, 'row', scatter_dimension=0, tiled=True)  149 us
    reduce_scatter x1, waiting for transfers between devices, on_device(): lax.psum_scatter(grad_down_full, 'dp', scatter_dimension=0, tiled=True)  103 us
    psum x3, waiting for transfers between devices, col_total(): return lax.psum(matrix, 'col')  87.7 us
    psum x1, blocking collectives, on_device(): lax.psum((grad_joined, grad_out_part, grad_router, grad_gain1, grad_gain2...  67.6 us
    all_gather x2, waiting for transfers between devices, slot_collect(): return lax.all_gather(matrix, 'row', axis=0, tiled=True)  64.9 us
    psum x1, waiting for transfers between devices, on_device(): lax.psum((grad_joined, grad_out_part, grad_router, grad_gain1, grad_gain2...  63.4 us
    reduce_scatter x3, waiting for transfers between devices, head_share(): return lax.psum_scatter(matrix, 'row', scatter_dimension=0, tiled=True)  45.8 us
  transfers between devices with their start and end apart: 15, of which 15 were waited for; matrix products, arithmetic and copies ran while one was open for 9% of the time, Pallas kernels for 0%

commit v1 on v0

--- a/solution.py
+++ b/solution.py
@@ -2,6 +2,7 @@
 import jax.numpy as jnp
 from jax import lax
 from jax.sharding import PartitionSpec as P
+from jax.lax import psum
 
 D = 1024
 HEAD_DIM = 64
@@ -198,7 +199,8 @@
     resid_out = resid_mid + col_total(jnp.sum(gate_probs[:, :, None] * picked, axis=1))
     block_out = resid_out.astype(low)
     grad_top = cotangent.astype(f32)
-    grad_prob = lax.psum(jnp.sum(grad_top[:, None, :] * picked, axis=2), ("row", "col"))
+    load = jnp.sum(grad_top[:, None, :] * picked, axis=2)
+    grad_prob = psum(psum(load, axis_name="row"), axis_name="col")
     grad_chosen = gate_probs * (grad_prob - jnp.sum(gate_probs * grad_prob, axis=1, keepdims=True))
     expert_hits = (
         expert_ids[:, :, None] == jnp.arange(EXPERTS, dtype=jnp.int32)[None, None, :]

time: 1190 us -> 1180 us (level)
    psum x1 -> x2, blocking collectives: 32.4 us -> 23.1 us  [on_device(): grad_prob = psum(psum(load, axis_name='row'), axis_name='col')]
where the time goes in v1:
time: 1180 us; the launch traced here: 1170 us
  waiting for transfers between devices  730 us (62%)
  blocking collectives  161 us (14%)
  local copies, waits for them, and re-layouts  157 us (13%)
  matrix products  66.7 us (6%)
  other arithmetic  44.7 us (4%)
  between operations  14.9 us (1%)
    reduce_scatter x2, waiting for transfers between devices, slot_share(): return lax.psum_scatter(matrix, 'row', scatter_dimension=0, tiled=True)  149 us
    reduce_scatter x1, waiting for transfers between devices, on_device(): lax.psum_scatter(grad_both_full, 'dp', scatter_dimension=0, tiled=True)  149 us
    reduce_scatter x1, waiting for transfers between devices, on_device(): lax.psum_scatter(grad_down_full, 'dp', scatter_dimension=0, tiled=True)  103 us
    psum x3, waiting for transfers between devices, col_total(): return lax.psum(matrix, 'col')  87.6 us
    psum x1, blocking collectives, on_device(): lax.psum((grad_joined, grad_out_part, grad_router, grad_gain1, grad_gain2...  67.6 us
    all_gather x2, waiting for transfers between devices, slot_collect(): return lax.all_gather(matrix, 'row', axis=0, tiled=True)  64.9 us
    psum x1, waiting for transfers between devices, on_device(): lax.psum((grad_joined, grad_out_part, grad_router, grad_gain1, grad_gain2...  63.4 us
    reduce_scatter x3, waiting for transfers between devices, head_share(): return lax.psum_scatter(matrix, 'row', scatter_dimension=0, tiled=True)  45.8 us
  transfers between devices with their start and end apart: 15, of which 15 were waited for; matrix products, arithmetic and copies ran while one was open for 9% of the time, Pallas kernels for 0%

profile of v1, /device:TPU:0, one launch (start us, length us, event | category | flops | bytes accessed | tf_op | source)
XLA Modules:
  0.0 1174.9 jit_solution(314940548058402314)
XLA Ops:
  8.4 11.9 %psum.112 = f32[512]{0:T(512)S(1)} all-reduce(f32[512]{0:T(512)S(1)} %fusion.10), channel_id=1, replica_groups=mesh['dp'=16,'row'=4,'col'=2] {'row'}, use_global_device_ids=true, to_apply=%region_1.0 | all-reduce | flops 512 | bytes 4096 | tf_op jit(solution)/shard_map/psum | solution.py:52
  28.1 9.2 reduce-window.6
  38.9 15.5 %scatter_custom_fusion = s32[5120]{0:T(1024)S(1)} fusion(s32[4096]{0:T(1024)S(1)} %bitcast.134, s32[4096]{0:T(1024)S(1)} %iota.35, s32[]{:T(128)} %constant.152.clone.1), kind=kCustom, calls=%fused_computation.130 | custom fusion | bytes 20484 | tf_op jit(solution)/shard_map/scatter | solution.py:46
  59.9 13.5 %all_gather.15 = bf16[512,512]{1,0:T(8,128)(2,1)S(1)} all-gather(bf16[128,512]{1,0:T(8,128)(2,1)S(1)} %pad_maximum_fusion.3), channel_id=1, replica_groups=mesh['dp'=16,'row'=4,'col'=2] {'row'}, dimensions={0}, use_global_device_ids=true | all-gather | bytes 655360 | tf_op jit(solution)/shard_map/all_gather | solution.py:64
  76.7 13.0 %all_gather.16 = bf16[512,512]{0,1:T(8,128)(2,1)S(1)} all-gather(bf16[128,512]{0,1:T(8,128)(2,1)S(1)} %bitcast.123), channel_id=1, replica_groups=mesh['dp'=16,'row'=4,'col'=2] {'row'}, dimensions={0}, use_global_device_ids=true | all-gather | bytes 655360 | tf_op jit(solution)/shard_map/all_gather | solution.py:64
  101.2 26.6 %all-reduce.11.cloned.1.call-done = f32[512,256]{1,0:T(8,128)} async-done(((f32[512,256]{1,0:T(8,128)}), f32[512,256]{1,0:T(8,128)}) %all-reduce.11.cloned.1.call-update) | async-done | bytes 524304 | tf_op jit(solution)/shard_map/psum | solution.py:56
  129.0 10.7 psum.114
  140.5 18.2 %gather_fusion = bf16[5120,256]{1,0:T(8,128)(2,1)S(1)} fusion(bf16[513,256]{1,0:T(8,128)(2,1)S(1)} %concatenate.45, s32[5120]{0:T(1024)S(1)} %get-tuple-element.121), kind=kCustom, calls=%fused_computation.2 | custom fusion | bytes 5263360 | tf_op jit(solution)/shard_map/jit(_take)/gather | solution.py:185
  158.7 8.1 fusion.3
  168.4 95.0 %reduce-scatter.10.cloned.1.call-done = f32[1280,512]{1,0:T(8,128)} async-done(((f32[5120,512]{1,0:T(8,128)}), f32[1280,512]{1,0:T(8,128)}) %reduce-scatter.10.cloned.1.call-update) | async-done | bytes 2621456 | tf_op jit(solution)/shard_map/reduce_scatter | solution.py:68
  267.0 39.8 %all-reduce.13.cloned.1.call-done = f32[512,32]{0,1:T(8,128)} async-done(((f32[512,32]{0,1:T(8,128)}), f32[512,32]{0,1:T(8,128)}) %all-reduce.13.cloned.1.call-update) | async-done | bytes 65552 | tf_op jit(solution)/shard_map/psum | solution.py:180
  306.8 28.9 %gather_fusion.2 = f32[4096]{0:T(1024)S(1)} fusion(f32[512,32]{0,1:T(8,128)} %all-reduce.13.cloned.1.call-done, s32[4096]{0:T(1024)S(1)} %reshape.440), kind=kCustom, calls=%fused_computation.4 | custom fusion | bytes 65536 | tf_op jit(solution)/shard_map/jit(take_along_axis)/gather | solution.py:181
  350.3 18.6 %gather_fusion.3 = f32[4096,256]{1,0:T(8,128)} fusion(f32[5120,256]{1,0:T(8,128)} %bitcast.103, s32[4096]{0:T(1024)S(1)} %broadcast_clamp_fusion.1), kind=kCustom, calls=%fused_computation.clone | custom fusion | bytes 8404992 | tf_op jit(solution)/shard_map/jit(_take)/gather | solution.py:198
  372.0 14.9 %psum.118 = f32[512,8]{0,1:T(8,128)S(1)} all-reduce(f32[512,8]{0,1:T(8,128)S(1)} %copy.81), channel_id=1, replica_groups=mesh['dp'=16,'row'=4,'col'=2] {'row'}, use_global_device_ids=true, to_apply=%region_22.24 | all-reduce | flops 4096 | bytes 32768 | tf_op jit(solution)/shard_map/psum | solution.py:203
  386.9 8.1 psum.119
  397.3 20.9 %gather_fusion.1 = bf16[5120,256]{1,0:T(8,128)(2,1)} fusion(bf16[4097,256]{1,0:T(8,128)(2,1)S(1)} %concatenate.47, s32[5120]{0:T(1024)S(1)} %get-tuple-element.120), kind=kCustom, calls=%fused_computation.3 | custom fusion | bytes 5263360 | tf_op jit(solution)/shard_map/jit(_take)/gather | solution.py:212
  425.2 54.4 %reduce-scatter.12.cloned.1.call-done = f32[1280,256]{1,0:T(8,128)} async-done(((f32[5120,256]{1,0:T(8,128)}), f32[1280,256]{1,0:T(8,128)}) %reduce-scatter.12.cloned.1.call-update) | async-done | bytes 1310736 | tf_op jit(solution)/shard_map/reduce_scatter | solution.py:68
  482.8 56.9 %all-gather.6.cloned.1.call-done = bf16[5120,512]{1,0:T(8,128)(2,1)} async-done(((bf16[1280,512]{1,0:T(8,128)(2,1)}), bf16[5120,512]{1,0:T(8,128)(2,1)}) %all-gather.6.cloned.1.call-update) | async-done | bytes 5242896 | tf_op jit(solution)/shard_map/all_gather | solution.py:72
  539.7 10.1 fusion.64
  549.8 18.6 %gather_fusion.4 = f32[4096,256]{1,0:T(8,128)} fusion(f32[5120,256]{1,0:T(8,128)} %bitcast.102, s32[4096]{0:T(1024)S(1)} %broadcast_clamp_fusion.1), kind=kCustom, calls=%fused_computation.1.clone | custom fusion | bytes 8404992 | tf_op jit(solution)/shard_map/jit(_take)/gather | solution.py:240
  576.4 35.5 %all-reduce.15.cloned.1.call-done = f32[512,256]{1,0:T(8,128)} async-done(((f32[512,256]{1,0:T(8,128)}), f32[512,256]{1,0:T(8,128)}) %all-reduce.15.cloned.1.call-update) | async-done | bytes 524304 | tf_op jit(solution)/shard_map/psum | solution.py:56
  614.7 10.6 psum.120
  628.5 22.2 %reduce-scatter.14.cloned.1.call-done = f32[128,512]{1,0:T(8,128)} async-done(((f32[512,512]{1,0:T(8,128)}), f32[128,512]{1,0:T(8,128)}) %reduce-scatter.14.cloned.1.call-update) | async-done | bytes 262160 | tf_op jit(solution)/shard_map/reduce_scatter | solution.py:60
  659.9 22.5 %reduce-scatter.16.cloned.1.call-done = f32[128,512]{0,1:T(8,128)} async-done(((f32[512,512]{0,1:T(8,128)}), f32[128,512]{0,1:T(8,128)}) %reduce-scatter.16.cloned.1.call-update) | async-done | bytes 262160 | tf_op jit(solution)/shard_map/reduce_scatter | solution.py:60
  685.0 25.7 %all-gather.8.cloned.1.call-done = bf16[512,1024]{0,1:T(8,128)(2,1)} async-done(((bf16[128,1024]{0,1:T(8,128)(2,1)}), bf16[512,1024]{0,1:T(8,128)(2,1)}) %all-gather.8.cloned.1.call-update) | async-done | bytes 1048592 | tf_op jit(solution)/shard_map/all_gather | solution.py:64
  718.8 9.1 fusion.2
  736.4 25.5 %all-reduce.19.cloned.1.call-done = (f32[512,256]{1,0:T(8,128)}, f32[512,256]{1,0:T(8,128)}) async-done(((f32[512,256]{1,0:T(8,128)}, f32[512,256]{1,0:T(8,128)}), (f32[512,256]{1,0:T(8,128)}, f32[512,256]{1,0:T(8,128)})) %all-reduce.19.cloned.1.call-update) | async-done | bytes 1048592 | tf_op jit(solution)/shard_map/psum | solution.py:56
  763.3 10.7 psum.122
  773.9 67.6 %all-reduce.2 = (f32[256,32]{0,1:T(8,128)}, f32[256]{0:T(256)}, f32[256]{0:T(256)}) all-reduce(f32[256,32]{0,1:T(8,128)S(1)} %fusion.66, f32[256]{0:T(256)S(1)} %get-tuple-element.73, f32[256]{0:T(256)S(1)} %copy-done.50), channel_id=1, replica_groups=mesh['dp'=16,'row'=4,'col'=2] {'dp'}, use_global_device_ids=true, to_apply=%region_38.40 | all-reduce | flops 8704 | bytes 69632 | tf_op jit(solution)/shard_map/psum | solution.py:310
  845.4 63.4 %all-reduce.17.cloned.1.call-done = (f32[256,1024]{1,0:T(8,128)}, f32[512,256]{1,0:T(8,128)}) async-done(((f32[256,1024]{1,0:T(8,128)}, f32[512,256]{1,0:T(8,128)}), (f32[256,1024]{1,0:T(8,128)}, f32[512,256]{1,0:T(8,128)})) %all-reduce.17.cloned.1.call-update) | async-done | bytes 1572880 | tf_op jit(solution)/shard_map/psum | solution.py:310
  912.6 149.2 %reduce-scatter.18.cloned.1.call-done = f32[2,256,512]{2,1,0:T(8,128)} async-done(((f32[32,256,512]{2,1,0:T(8,128)}), f32[2,256,512]{2,1,0:T(8,128)}) %reduce-scatter.18.cloned.1.call-update) | async-done | bytes 1048592 | tf_op jit(solution)/shard_map/reduce_scatter | solution.py:234
  1064.0 103.5 %reduce-scatter.20.cloned.1.call-done = f32[2,256,256]{2,1,0:T(8,128)} async-done(((f32[32,256,256]{2,1,0:T(8,128)}), f32[2,256,256]{2,1,0:T(8,128)}) %reduce-scatter.20.cloned.1.call-update) | async-done | bytes 524304 | tf_op jit(solution)/shard_map/reduce_scatter | solution.py:235
  (249 shorter events, 121.5 us)
Async XLA Ops:
  7.2 83.3 %copy-start = (bf16[512,256]{1,0:T(8,128)(2,1)S(1)}, bf16[512,256]{1,0:T(8,128)(2,1)}, u32[]{:S(2)}) copy-start(bf16[512,256]{1,0:T(8,128)(2,1)} %param.24) | copy-start | bytes 786436
  7.2 49.4 %reduce-scatter.8.cloned.1.call-start = ((), (), s32[]{:S(2)}) async-start(), calls=%async_computation.7 | async-start | bytes 2621440 | tf_op jit(solution)/shard_map/reduce_scatter | solution.py:60
  27.2 100.6 %all-reduce.11.cloned.1.call-start = ((), (), s32[]{:S(2)}) async-start(), calls=%async_computation.8 | async-start | bytes 1048576 | tf_op jit(solution)/shard_map/psum | solution.py:56
  91.7 171.7 %reduce-scatter.10.cloned.1.call-start = ((), (), s32[]{:S(2)}) async-start(), calls=%async_computation.10 | async-start | bytes 13107200 | tf_op jit(solution)/shard_map/reduce_scatter | solution.py:68
  96.5 31.3 %copy-start.9 = (bf16[512,256]{1,0:T(8,128)(2,1)S(1)}, bf16[512,256]{1,0:T(8,128)(2,1)}, u32[]{:S(2)}) copy-start(bf16[512,256]{1,0:T(8,128)(2,1)} %param.16) | copy-start | bytes 786436
  96.5 43.8 %copy-start.45 = (f32[256]{0:T(256)S(1)}, f32[256]{0:T(256)}, u32[]{:S(2)}) copy-start(f32[256]{0:T(256)} %param.25) | copy-start | bytes 3076
  166.8 100.1 %copy-start.27 = (bf16[512,256]{1,0:T(8,128)(2,1)S(1)}, bf16[512,256]{1,0:T(8,128)(2,1)}, u32[]{:S(2)}) copy-start(bf16[512,256]{1,0:T(8,128)(2,1)} %param.19) | copy-start | bytes 786436
  166.8 140.0 %all-reduce.13.cloned.1.call-start = ((), (), s32[]{:S(2)}) async-start(), calls=%async_computation.9 | async-start | bytes 131072 | tf_op jit(solution)/shard_map/psum | solution.py:180
  168.3 175.8 %all-gather.4.cloned.1.call-start = ((), (), s32[]{:S(2)}) async-start(), calls=%async_computation.11 | async-start | bytes 3276800 | tf_op jit(solution)/shard_map/all_gather | solution.py:72
  266.3 213.3 %reduce-scatter.12.cloned.1.call-start = ((), (), s32[]{:S(2)}) async-start(), calls=%async_computation.12 | async-start | bytes 6553600 | tf_op jit(solution)/shard_map/reduce_scatter | solution.py:68
  425.2 54.5 %copy-start.8 = (f32[1280,512]{1,0:T(8,128)S(1)}, f32[1280,512]{1,0:T(8,128)}, u32[]{:S(2)}) copy-start(f32[1280,512]{1,0:T(8,128)} %reduce-scatter.10.cloned.1.call-done) | copy-start | bytes 7864324
  425.2 114.5 %all-gather.6.cloned.1.call-start = ((), (), s32[]{:S(2)}) async-start(), calls=%async_computation.13 | async-start | bytes 6553600 | tf_op jit(solution)/shard_map/all_gather | solution.py:72
  482.7 129.2 %all-reduce.15.cloned.1.call-start = ((), (), s32[]{:S(2)}) async-start(), calls=%async_computation.14 | async-start | bytes 1048576 | tf_op jit(solution)/shard_map/psum | solution.py:56
  568.4 43.5 %copy-start.7 = (f32[512,256]{1,0:T(8,128)S(1)}, f32[512,256]{1,0:T(8,128)}, u32[]{:S(2)}) copy-start(f32[512,256]{1,0:T(8,128)} %copy-done.6) | copy-start | bytes 1572868
  568.4 43.5 %copy-start.46 = (f32[256]{0:T(256)S(1)}, f32[256]{0:T(256)}, u32[]{:S(2)}) copy-start(f32[256]{0:T(256)} %param.25) | copy-start | bytes 3076
  568.4 56.9 %copy-start.49 = (f32[512]{0:T(512)S(1)}, f32[512]{0:T(512)}, u32[]{:S(2)}) copy-start(f32[512]{0:T(512)} %get-tuple-element.124) | copy-start | bytes 6148
  576.3 74.5 %reduce-scatter.14.cloned.1.call-start = ((), (), s32[]{:S(2)}) async-start(), calls=%async_computation.15 | async-start | bytes 1310720 | tf_op jit(solution)/shard_map/reduce_scatter | solution.py:60
  576.4 48.9 %copy-start.36 = (bf16[512,32]{0,1:T(8,128)(2,1)}, bf16[512,32]{0,1:T(8,128)(2,1)S(1)}, u32[]{:S(2)}) copy-start(bf16[512,32]{0,1:T(8,128)(2,1)S(1)} %select_reduce_fusion) | copy-start | bytes 98308
  625.3 29.1 %copy-start.2 = (f32[8,128,512]{2,1,0:T(8,128)S(1)}, f32[8,128,512]{2,1,0:T(8,128)}, u32[]{:S(2)}) copy-start(f32[8,128,512]{2,1,0:T(8,128)} %copy-done.1) | copy-start | bytes 6291460
  628.2 54.2 %reduce-scatter.16.cloned.1.call-start = ((), (), s32[]{:S(2)}) async-start(), calls=%async_computation.16 | async-start | bytes 1310720 | tf_op jit(solution)/shard_map/reduce_scatter | solution.py:60
  658.8 52.0 %copy-start.23 = (bf16[256,1024]{1,0:T(8,128)(2,1)S(1)}, bf16[256,1024]{1,0:T(8,128)(2,1)}, u32[]{:S(2)}) copy-start(bf16[256,1024]{1,0:T(8,128)(2,1)} %copy-done.22) | copy-start | bytes 1572868
  658.8 51.9 %all-gather.8.cloned.1.call-start = ((), (), s32[]{:S(2)}) async-start(), calls=%async_computation.17 | async-start | bytes 1310720 | tf_op jit(solution)/shard_map/all_gather | solution.py:64
  685.0 30.8 %copy-start.43 = (f32[512]{0:T(512)S(1)}, f32[512]{0:T(512)}, u32[]{:S(2)}) copy-start(f32[512]{0:T(512)} %copy-done.42) | copy-start | bytes 6148
  685.0 30.8 %copy-start.44 = (f32[256]{0:T(256)S(1)}, f32[256]{0:T(256)}, u32[]{:S(2)}) copy-start(f32[256]{0:T(256)} %param.20) | copy-start | bytes 3076
  685.0 76.9 %all-reduce.19.cloned.1.call-start = ((), (), s32[]{:S(2)}) async-start(), calls=%async_computation.21 | async-start | bytes 2097152 | tf_op jit(solution)/shard_map/psum | solution.py:56
  713.3 195.5 %all-reduce.17.cloned.1.call-start = ((), (), s32[]{:S(2)}) async-start(), calls=%async_computation.20 | async-start | bytes 3145728 | tf_op jit(solution)/shard_map/psum | solution.py:310
  718.7 343.0 %reduce-scatter.18.cloned.1.call-start = ((), (), s32[]{:S(2)}) async-start(), calls=%async_computation.18 | async-start | bytes 17825792 | tf_op jit(solution)/shard_map/reduce_scatter | solution.py:234
  727.9 439.6 %reduce-scatter.20.cloned.1.call-start = ((), (), s32[]{:S(2)}) async-start(), calls=%async_computation.19 | async-start | bytes 8912896 | tf_op jit(solution)/shard_map/reduce_scatter | solution.py:235
  735.3 38.6 %copy-start.50 = (f32[256]{0:T(256)S(1)}, f32[256]{0:T(256)}, u32[]{:S(2)}) copy-start(f32[256]{0:T(256)} %get-tuple-element.71) | copy-start | bytes 3076
  735.3 108.1 %copy-start.47 = (f32[512]{0:T(512)S(1)}, f32[512]{0:T(512)}, u32[]{:S(2)}) copy-start(f32[512]{0:T(512)} %get-tuple-element.122) | copy-start | bytes 6148
  736.3 107.1 %copy-start.14 = (f32[512,256]{1,0:T(8,128)S(1)}, f32[512,256]{1,0:T(8,128)}, u32[]{:S(2)}) copy-start(f32[512,256]{1,0:T(8,128)} %copy-done.13) | copy-start | bytes 1572868
  908.8 258.7 %copy-start.33 = (f32[512,256]{1,0:T(8,128)S(1)}, f32[512,256]{1,0:T(8,128)}, u32[]{:S(2)}) copy-start(f32[512,256]{1,0:T(8,128)} %get-tuple-element.139) | copy-start | bytes 1572868
  (35 other events, 262.9 us)
Sparse Core Ops, SparseCore 0:
  27.3 29.1 reduce-scatter.7
  91.8 35.9 all-reduce.10
  166.9 96.3 reduce-scatter.9
  266.1 40.6 all-reduce.12
  308.4 35.6 all-gather.3
  425.3 54.2 reduce-scatter.11
  482.8 56.7 all-gather.5
  576.4 35.5 all-reduce.14
  628.3 22.3 reduce-scatter.13
  658.9 23.4 reduce-scatter.15
  685.1 25.5 all-gather.7
  714.2 47.6 all-reduce.18
  765.3 143.4 all-reduce.16
  913.0 148.7 reduce-scatter.17
  1067.2 100.3 reduce-scatter.19
